TPU v7x, 32 devices: a whole 2x2x4 slice. The times are simulated.
32 devices in a mesh: groups: 2 (over y), branch: 4 (over z), head: 4 (over x, core).
Axes of the slice: x: 2, y: 2, z: 4, core: 2. Of those that a mesh axis runs over, the one named last changes fastest.
Arguments:
- queries: bfloat16 [1536, 5120], P(('groups', 'branch'), 'head'), parts along dimension 0, may hold values from -6 to 6
- key_states: bfloat16 [1536, 1024], P(('groups', 'branch'), 'head'), parts along dimension 0, may hold values from -6 to 6
- value_states: bfloat16 [1536, 1024], P(('groups', 'branch'), 'head'), parts along dimension 0, may hold values from -6 to 6
- cotangent: bfloat16 [1536, 5120], P(('groups', 'branch'), 'head'), parts along dimension 0, may hold values from -48 to 48
- key_weight: bfloat16 [5120, 1024], P(None, 'head'), may hold values from -0.078125 to 0.078125
- value_weight: bfloat16 [5120, 1024], P(None, 'head'), may hold values from -0.078125 to 0.078125
- leaf_length: int32 [8], P(('groups', 'branch')), parts along dimension 0, may hold values from 32 to 128, as said below
Outputs:
- d_query: bfloat16 [1536, 5120], P(('groups', 'branch'), 'head'), parts along dimension 0
- d_input: bfloat16 [1536, 5120], P(('groups', 'branch', 'head')), parts along dimension 0
There are 2 independent parts, one for each index of `groups`. A program takes and returns all parts, laid end to end along the dimension named above; an argument that names none is the same for every part. Nothing has to cross between parts.
Inputs may be any that keep to these rules, and one draw needn't show every extreme that they name: `leaf_length`: some leaf has exactly 128 live tokens.
All inputs are finite; a program needn't handle non-finite values.
Results may differ from a plain program's by a relative error of at most 0.012.
The roundings to bfloat16 on the way count: a program that leaves them out, or rounds other values in their place, can miss the bound.
Values may be sent and summed in bfloat16 or wider, within the bound.
A program may use at most 64 MiB of HBM per device.

v0:
```python
import jax
import jax.numpy as jnp
from jax import lax
from jax.sharding import PartitionSpec as P

HD = 128
ANC = 32


def swapped(value, axis, apart):
    return lax.ppermute(value, axis, [(i, i ^ 1 << apart) for i in range(lax.axis_size(axis))])


def local(queries, key_states, value_states, cotangent, key_weight, value_weight, leaf_length):
    levels = lax.axis_size("branch").bit_length() - 1
    branch_pos = lax.axis_index("branch")
    row_count = queries.shape[0]
    leaf_rows = row_count - levels * ANC
    kv_cols = key_states.shape[1]
    kv_local = kv_cols // HD
    group_size = queries.shape[1] // kv_cols
    score_scale = HD ** (-0.5)
    pair_cols = 2 * kv_cols
    joined = jnp.concatenate([key_states, value_states], axis=1)
    own_anc = joined[leaf_rows:].reshape(1, levels, ANC, pair_cols)
    segments = []
    gathered = lax.all_gather(own_anc, "branch", axis=0, tiled=True)
    for level_no in range(1, levels + 1):
        span_rows = 2**level_no
        first_row = branch_pos // span_rows * span_rows
        piece_rows = lax.dynamic_slice_in_dim(gathered[:, level_no - 1], first_row, span_rows, 0)
        segments.append(piece_rows.reshape(span_rows * ANC, pair_cols))
    key_set = jnp.concatenate(segments[::-1] + [joined[:leaf_rows]], axis=0)
    key_count = key_set.shape[0]
    key_level = jnp.concatenate(
        [jnp.full((2**level_no * ANC,), level_no, jnp.int32) for level_no in range(levels, 0, -1)]
        + [jnp.zeros((leaf_rows,), jnp.int32)]
    )
    key_place = jnp.concatenate(
        [jnp.arange(2**level_no * ANC, dtype=jnp.int32) for level_no in range(levels, 0, -1)]
        + [jnp.arange(leaf_rows, dtype=jnp.int32)]
    )
    query_level = jnp.concatenate(
        [jnp.zeros((leaf_rows,), jnp.int32)]
        + [jnp.full((ANC,), level_no, jnp.int32) for level_no in range(1, levels + 1)]
    )
    query_place = jnp.concatenate(
        [jnp.arange(leaf_rows, dtype=jnp.int32)]
        + [
            branch_pos % 2**level_no * ANC + jnp.arange(ANC, dtype=jnp.int32)
            for level_no in range(1, levels + 1)
        ]
    )
    allowed = (key_level[None, :] > query_level[:, None]) | (
        key_level[None, :] == query_level[:, None]
    ) & (key_place[None, :] <= query_place[:, None])
    live_rows = (query_level > 0) | (query_place < leaf_length[0])
    d_masked = jnp.where(live_rows[:, None], cotangent, jnp.zeros_like(cotangent))
    key_part = key_set[:, :kv_cols].reshape(key_count, kv_local, HD)
    value_part = key_set[:, kv_cols:].reshape(key_count, kv_local, HD)
    query_heads = jnp.transpose(queries.reshape(row_count, kv_local, group_size, HD), (2, 0, 1, 3))
    d_heads = jnp.transpose(d_masked.reshape(row_count, kv_local, group_size, HD), (2, 0, 1, 3))

    def one_head(totals, inputs):
        grad_key, grad_value = totals
        query_one, d_one = inputs
        scores = (
            jnp.einsum("rgd,kgd->grk", query_one, key_part, preferred_element_type=jnp.float32)
            * score_scale
        )
        scores = jnp.where(allowed[None], scores, -jnp.inf)
        row_max = jnp.max(scores, axis=2, keepdims=True)
        exp_scores = jnp.exp(scores - row_max)
        attn_prob = exp_scores / jnp.sum(exp_scores, axis=2, keepdims=True)
        attn_bf = attn_prob.astype(jnp.bfloat16)
        attended = jnp.einsum(
            "grk,kgd->rgd", attn_bf, value_part, preferred_element_type=jnp.float32
        )
        row_delta = jnp.sum(d_one.astype(jnp.float32) * attended, axis=2)
        grad_prob = jnp.einsum(
            "rgd,kgd->grk", d_one, value_part, preferred_element_type=jnp.float32
        )
        grad_score = (attn_prob * (grad_prob - jnp.transpose(row_delta)[:, :, None])).astype(
            jnp.bfloat16
        )
        grad_query = (
            jnp.einsum("grk,kgd->rgd", grad_score, key_part, preferred_element_type=jnp.float32)
            * score_scale
        )
        grad_key = (
            grad_key
            + jnp.einsum("grk,rgd->kgd", grad_score, query_one, preferred_element_type=jnp.float32)
            * score_scale
        )
        grad_value = grad_value + jnp.einsum(
            "grk,rgd->kgd", attn_bf, d_one, preferred_element_type=jnp.float32
        )
        return ((grad_key, grad_value), grad_query.astype(jnp.bfloat16))

    zero_grads = jnp.zeros((key_count, kv_local, HD), jnp.float32)
    (grad_key, grad_value), query_grads = lax.scan(
        one_head, (zero_grads, zero_grads), (query_heads, d_heads)
    )
    d_query = jnp.transpose(query_grads, (1, 2, 0, 3)).reshape(row_count, queries.shape[1])
    grads = jnp.concatenate(
        [grad_key.reshape(key_count, kv_cols), grad_value.reshape(key_count, kv_cols)], axis=1
    )
    level_grads = [None] * levels
    offset = 0
    for level_no in range(levels, 0, -1):
        span_rows = 2**level_no * ANC
        level_grads[level_no - 1] = grads[offset : offset + span_rows].reshape(
            2**level_no, ANC, pair_cols
        )
        offset = offset + span_rows
    leaf_grads = grads[offset:]
    reduced = []
    for level_no in range(1, levels + 1):
        buffer_rows = level_grads[level_no - 1]
        for bit_no in range(level_no - 1, -1, -1):
            halves = buffer_rows.reshape(2, 2**bit_no, ANC, pair_cols)
            is_upper = branch_pos >> bit_no & 1 == 1
            kept_half = jnp.where(is_upper, halves[1], halves[0])
            sent_half = jnp.where(is_upper, halves[0], halves[1])
            buffer_rows = kept_half + swapped(sent_half, "branch", bit_no)
        reduced.append(buffer_rows[0])
    own_grads = jnp.concatenate([leaf_grads] + reduced, axis=0).astype(jnp.bfloat16)
    contract = (((1,), (1,)), ((), ()))
    key_term = lax.dot_general(
        own_grads[:, :kv_cols], key_weight, contract, preferred_element_type=jnp.float32
    )
    value_term = lax.dot_general(
        own_grads[:, kv_cols:], value_weight, contract, preferred_element_type=jnp.float32
    )
    d_input = lax.psum_scatter(
        (key_term + value_term).astype(jnp.bfloat16), "head", scatter_dimension=0, tiled=True
    )
    return (d_query, d_input)


def solution(mesh):
    placed = (
        P(("groups", "branch"), "head"),
        P(("groups", "branch"), "head"),
        P(("groups", "branch"), "head"),
        P(("groups", "branch"), "head"),
        P(None, "head"),
        P(None, "head"),
        P(("groups", "branch")),
    )
    return jax.shard_map(
        local,
        mesh=mesh,
        in_specs=placed,
        out_specs=(P(("groups", "branch"), "head"), P(("groups", "branch", "head"), None)),
        check_vma=False,
    )
```

profile of v0, /device:TPU:1, one launch (start us, length us, event | category | flops | bytes accessed | tf_op | source)
XLA Modules:
  0.0 148.1 jit_solution(8654078650703319271)
XLA Ops:
  7.3 1.1 constant_dynamic-update-slice_fusion.1
  9.9 13.3 %all_gather.3 = bf16[4,2,32,512]{3,2,0,1:T(8,128)(2,1)S(1)} all-gather(bf16[1,2,32,512]{3,2,0,1:T(8,128)(2,1)S(1)} %bitcast.149), channel_id=1, replica_groups=mesh['groups'=2,'branch'=4,'head'=4] {'branch'}, dimensions={0}, use_global_device_ids=true | all-gather | bytes 327680 | tf_op jit(solution)/shard_map/all_gather | solution.py:27
  24.2 1.1 broadcast_select_fusion
  25.3 1.1 copy.13
  26.4 2.1 %copy.16 = bf16[5,192,2,128]{3,1,2,0:T(8,128)(2,1)} copy(bf16[5,192,2,128]{1,3,0,2:T(8,128)(2,1)} %bitcast.143) | data formatting | bytes 983040
  28.6 2.1 %copy.11 = bf16[192,1280]{0,1:T(8,128)(2,1)} copy(bf16[192,1280]{1,0:T(8,128)(2,1)} %param.9) | data formatting | bytes 983040 | tf_op args[0]
  30.7 2.1 %copy.14 = bf16[5,192,2,128]{3,1,2,0:T(8,128)(2,1)} copy(bf16[5,192,2,128]{1,3,0,2:T(8,128)(2,1)} %bitcast.145) | data formatting | bytes 983040
  33.6 57.1 %while.15 = (s32[]{:T(128)}, f32[320,2,128]{2,0,1:T(8,128)S(1)}, f32[320,2,128]{2,0,1:T(8,128)}, bf16[5,192,2,128]{3,1,2,0:T(8,128)(2,1)}, bf16[5,192,2,128]{3,1...) while((s32[]{:T(128)}, f32[320,2,128]{2,0,1:T(8,128)S(1)}, ...), condition=%wide.region_4.5_spmd.clone, body=%wide.region_0.4_spmd.clone.sunk | while | flops 254833984 | bytes 5160615 | solution.py:101
  33.7 2.1 %fusion.109 = (f32[2,192]{1,0:T(2,128)S(1)}, f32[2,192,320]{2,1,0:T(8,128)}) fusion(bf16[320,2,128]{2,0,1:T(8,128)(2,1)} %get-tuple-element.261, pred[192,320]{1,0:T(8,128)(4,1)S(1)} %and_or_fusion.2, bf16[5,192,2,128]{3,1,2,0:T(8,128)(2,1)} %get-tuple-element.260, s32[]{:T(128)S(6)} %copy.36), kind=kOutput, calls=%fused_computation.72.clone.1 | convolution fusion | flops 31949120 | bytes 816644 | tf_op jit(solution)/shard_map/while/body/eval_jaxpr/sub | solution.py:73
  35.9 1.9 %fusion.110 = f32[192,2]{0,1:T(2,128)S(1)} fusion(bf16[320,2,128]{2,0,1:T(8,128)(2,1)S(1)} %get-tuple-element.263, bf16[5,192,2,128]{3,1,2,0:T(8,128)(2,1)} %get-tuple-element.262, s32[]{:T(128)S(6)} %copy.36, f32[2,192]{1,0:T(2,128)S(1)} %get-tuple-element.226, bf16[320,2,128]{2,0,1:T(8,128)(2,1)} %get-tuple-element.261, ...), kind=kOutput, calls=%fused_computation.18.clone.1 | convolution fusion | flops 63676736 | bytes 589824 | tf_op jit(solution)/shard_map/while/body/eval_jaxpr/grk,kgd->rgd/dot_general | solution.py:76
  37.8 1.4 fusion.111
  39.2 2.7 %fusion.113 = f32[320,2,128]{2,0,1:T(8,128)} fusion(f32[320,2,128]{2,0,1:T(8,128)} %get-tuple-element.244, pred[]{:T(512)S(6)} %compare.9, bf16[5,192,2,128]{3,1,2,0:T(8,128)(2,1)} %get-tuple-element.262, s32[]{:T(128)S(6)} %copy.36, f32[2,192]{1,0:T(2,128)S(1)} %get-tuple-element.226, bf16[320,2,128]{2,0,1:T(8,128)(2,1)} %get-tuple-element.261, ...), kind=kOutput, calls=%fused_computation.10.clone.1 | convolution fusion | flops 63693504 | bytes 1080320 | tf_op jit(solution)/shard_map/while/body/eval_jaxpr/grk,rgd->kgd/dot_general | solution.py:95
  41.9 1.2 fusion.112
  43.1 1.8 %fusion.114 = bf16[5,192,2,128]{3,1,2,0:T(8,128)(2,1)} fusion(bf16[5,192,2,128]{3,1,2,0:T(8,128)(2,1)} %get-tuple-element.245, s32[]{:T(128)S(6)} %copy.36, bf16[2,192,320]{2,1,0:T(8,128)(2,1)S(1)} %fusion.111, bf16[320,2,128]{2,0,1:T(8,128)(2,1)} %get-tuple-element.261), kind=kOutput, calls=%fused_computation.20.clone.1 | convolution fusion | flops 31555584 | bytes 507908 | tf_op jit(solution)/shard_map/while/body/eval_jaxpr/grk,kgd->rgd/dot_general | solution.py:87
  45.1 2.1 %fusion.109 = (f32[2,192]{1,0:T(2,128)S(1)}, f32[2,192,320]{2,1,0:T(8,128)}) fusion(bf16[320,2,128]{2,0,1:T(8,128)(2,1)} %get-tuple-element.261, pred[192,320]{1,0:T(8,128)(4,1)S(1)} %and_or_fusion.2, bf16[5,192,2,128]{3,1,2,0:T(8,128)(2,1)} %get-tuple-element.260, s32[]{:T(128)S(6)} %copy.36), kind=kOutput, calls=%fused_computation.72.clone.1 | convolution fusion | flops 31949120 | bytes 816644 | tf_op jit(solution)/shard_map/while/body/eval_jaxpr/sub | solution.py:73
  47.2 1.9 %fusion.110 = f32[192,2]{0,1:T(2,128)S(1)} fusion(bf16[320,2,128]{2,0,1:T(8,128)(2,1)S(1)} %get-tuple-element.263, bf16[5,192,2,128]{3,1,2,0:T(8,128)(2,1)} %get-tuple-element.262, s32[]{:T(128)S(6)} %copy.36, f32[2,192]{1,0:T(2,128)S(1)} %get-tuple-element.226, bf16[320,2,128]{2,0,1:T(8,128)(2,1)} %get-tuple-element.261, ...), kind=kOutput, calls=%fused_computation.18.clone.1 | convolution fusion | flops 63676736 | bytes 589824 | tf_op jit(solution)/shard_map/while/body/eval_jaxpr/grk,kgd->rgd/dot_general | solution.py:76
  49.1 1.4 fusion.111
  50.5 2.9 %fusion.113 = f32[320,2,128]{2,0,1:T(8,128)} fusion(f32[320,2,128]{2,0,1:T(8,128)} %get-tuple-element.244, pred[]{:T(512)S(6)} %compare.9, bf16[5,192,2,128]{3,1,2,0:T(8,128)(2,1)} %get-tuple-element.262, s32[]{:T(128)S(6)} %copy.36, f32[2,192]{1,0:T(2,128)S(1)} %get-tuple-element.226, bf16[320,2,128]{2,0,1:T(8,128)(2,1)} %get-tuple-element.261, ...), kind=kOutput, calls=%fused_computation.10.clone.1 | convolution fusion | flops 63693504 | bytes 1080320 | tf_op jit(solution)/shard_map/while/body/eval_jaxpr/grk,rgd->kgd/dot_general | solution.py:95
  53.3 1.2 fusion.112
  54.6 1.8 %fusion.114 = bf16[5,192,2,128]{3,1,2,0:T(8,128)(2,1)} fusion(bf16[5,192,2,128]{3,1,2,0:T(8,128)(2,1)} %get-tuple-element.245, s32[]{:T(128)S(6)} %copy.36, bf16[2,192,320]{2,1,0:T(8,128)(2,1)S(1)} %fusion.111, bf16[320,2,128]{2,0,1:T(8,128)(2,1)} %get-tuple-element.261), kind=kOutput, calls=%fused_computation.20.clone.1 | convolution fusion | flops 31555584 | bytes 507908 | tf_op jit(solution)/shard_map/while/body/eval_jaxpr/grk,kgd->rgd/dot_general | solution.py:87
  56.5 2.1 %fusion.109 = (f32[2,192]{1,0:T(2,128)S(1)}, f32[2,192,320]{2,1,0:T(8,128)}) fusion(bf16[320,2,128]{2,0,1:T(8,128)(2,1)} %get-tuple-element.261, pred[192,320]{1,0:T(8,128)(4,1)S(1)} %and_or_fusion.2, bf16[5,192,2,128]{3,1,2,0:T(8,128)(2,1)} %get-tuple-element.260, s32[]{:T(128)S(6)} %copy.36), kind=kOutput, calls=%fused_computation.72.clone.1 | convolution fusion | flops 31949120 | bytes 816644 | tf_op jit(solution)/shard_map/while/body/eval_jaxpr/sub | solution.py:73
  58.6 1.9 %fusion.110 = f32[192,2]{0,1:T(2,128)S(1)} fusion(bf16[320,2,128]{2,0,1:T(8,128)(2,1)S(1)} %get-tuple-element.263, bf16[5,192,2,128]{3,1,2,0:T(8,128)(2,1)} %get-tuple-element.262, s32[]{:T(128)S(6)} %copy.36, f32[2,192]{1,0:T(2,128)S(1)} %get-tuple-element.226, bf16[320,2,128]{2,0,1:T(8,128)(2,1)} %get-tuple-element.261, ...), kind=kOutput, calls=%fused_computation.18.clone.1 | convolution fusion | flops 63676736 | bytes 589824 | tf_op jit(solution)/shard_map/while/body/eval_jaxpr/grk,kgd->rgd/dot_general | solution.py:76
  60.6 1.4 fusion.111
  61.9 2.9 %fusion.113 = f32[320,2,128]{2,0,1:T(8,128)} fusion(f32[320,2,128]{2,0,1:T(8,128)} %get-tuple-element.244, pred[]{:T(512)S(6)} %compare.9, bf16[5,192,2,128]{3,1,2,0:T(8,128)(2,1)} %get-tuple-element.262, s32[]{:T(128)S(6)} %copy.36, f32[2,192]{1,0:T(2,128)S(1)} %get-tuple-element.226, bf16[320,2,128]{2,0,1:T(8,128)(2,1)} %get-tuple-element.261, ...), kind=kOutput, calls=%fused_computation.10.clone.1 | convolution fusion | flops 63693504 | bytes 1080320 | tf_op jit(solution)/shard_map/while/body/eval_jaxpr/grk,rgd->kgd/dot_general | solution.py:95
  64.8 1.2 fusion.112
  66.0 1.8 %fusion.114 = bf16[5,192,2,128]{3,1,2,0:T(8,128)(2,1)} fusion(bf16[5,192,2,128]{3,1,2,0:T(8,128)(2,1)} %get-tuple-element.245, s32[]{:T(128)S(6)} %copy.36, bf16[2,192,320]{2,1,0:T(8,128)(2,1)S(1)} %fusion.111, bf16[320,2,128]{2,0,1:T(8,128)(2,1)} %get-tuple-element.261), kind=kOutput, calls=%fused_computation.20.clone.1 | convolution fusion | flops 31555584 | bytes 507908 | tf_op jit(solution)/shard_map/while/body/eval_jaxpr/grk,kgd->rgd/dot_general | solution.py:87
  67.9 2.1 %fusion.109 = (f32[2,192]{1,0:T(2,128)S(1)}, f32[2,192,320]{2,1,0:T(8,128)}) fusion(bf16[320,2,128]{2,0,1:T(8,128)(2,1)} %get-tuple-element.261, pred[192,320]{1,0:T(8,128)(4,1)S(1)} %and_or_fusion.2, bf16[5,192,2,128]{3,1,2,0:T(8,128)(2,1)} %get-tuple-element.260, s32[]{:T(128)S(6)} %copy.36), kind=kOutput, calls=%fused_computation.72.clone.1 | convolution fusion | flops 31949120 | bytes 816644 | tf_op jit(solution)/shard_map/while/body/eval_jaxpr/sub | solution.py:73
  70.1 1.9 %fusion.110 = f32[192,2]{0,1:T(2,128)S(1)} fusion(bf16[320,2,128]{2,0,1:T(8,128)(2,1)S(1)} %get-tuple-element.263, bf16[5,192,2,128]{3,1,2,0:T(8,128)(2,1)} %get-tuple-element.262, s32[]{:T(128)S(6)} %copy.36, f32[2,192]{1,0:T(2,128)S(1)} %get-tuple-element.226, bf16[320,2,128]{2,0,1:T(8,128)(2,1)} %get-tuple-element.261, ...), kind=kOutput, calls=%fused_computation.18.clone.1 | convolution fusion | flops 63676736 | bytes 589824 | tf_op jit(solution)/shard_map/while/body/eval_jaxpr/grk,kgd->rgd/dot_general | solution.py:76
  72.0 1.4 fusion.111
  73.4 2.9 %fusion.113 = f32[320,2,128]{2,0,1:T(8,128)} fusion(f32[320,2,128]{2,0,1:T(8,128)} %get-tuple-element.244, pred[]{:T(512)S(6)} %compare.9, bf16[5,192,2,128]{3,1,2,0:T(8,128)(2,1)} %get-tuple-element.262, s32[]{:T(128)S(6)} %copy.36, f32[2,192]{1,0:T(2,128)S(1)} %get-tuple-element.226, bf16[320,2,128]{2,0,1:T(8,128)(2,1)} %get-tuple-element.261, ...), kind=kOutput, calls=%fused_computation.10.clone.1 | convolution fusion | flops 63693504 | bytes 1080320 | tf_op jit(solution)/shard_map/while/body/eval_jaxpr/grk,rgd->kgd/dot_general | solution.py:95
  76.2 1.2 fusion.112
  77.4 1.8 %fusion.114 = bf16[5,192,2,128]{3,1,2,0:T(8,128)(2,1)} fusion(bf16[5,192,2,128]{3,1,2,0:T(8,128)(2,1)} %get-tuple-element.245, s32[]{:T(128)S(6)} %copy.36, bf16[2,192,320]{2,1,0:T(8,128)(2,1)S(1)} %fusion.111, bf16[320,2,128]{2,0,1:T(8,128)(2,1)} %get-tuple-element.261), kind=kOutput, calls=%fused_computation.20.clone.1 | convolution fusion | flops 31555584 | bytes 507908 | tf_op jit(solution)/shard_map/while/body/eval_jaxpr/grk,kgd->rgd/dot_general | solution.py:87
  79.4 2.1 %fusion.109 = (f32[2,192]{1,0:T(2,128)S(1)}, f32[2,192,320]{2,1,0:T(8,128)}) fusion(bf16[320,2,128]{2,0,1:T(8,128)(2,1)} %get-tuple-element.261, pred[192,320]{1,0:T(8,128)(4,1)S(1)} %and_or_fusion.2, bf16[5,192,2,128]{3,1,2,0:T(8,128)(2,1)} %get-tuple-element.260, s32[]{:T(128)S(6)} %copy.36), kind=kOutput, calls=%fused_computation.72.clone.1 | convolution fusion | flops 31949120 | bytes 816644 | tf_op jit(solution)/shard_map/while/body/eval_jaxpr/sub | solution.py:73
  81.5 1.9 %fusion.110 = f32[192,2]{0,1:T(2,128)S(1)} fusion(bf16[320,2,128]{2,0,1:T(8,128)(2,1)S(1)} %get-tuple-element.263, bf16[5,192,2,128]{3,1,2,0:T(8,128)(2,1)} %get-tuple-element.262, s32[]{:T(128)S(6)} %copy.36, f32[2,192]{1,0:T(2,128)S(1)} %get-tuple-element.226, bf16[320,2,128]{2,0,1:T(8,128)(2,1)} %get-tuple-element.261, ...), kind=kOutput, calls=%fused_computation.18.clone.1 | convolution fusion | flops 63676736 | bytes 589824 | tf_op jit(solution)/shard_map/while/body/eval_jaxpr/grk,kgd->rgd/dot_general | solution.py:76
  83.4 1.4 fusion.111
  84.8 2.9 %fusion.113 = f32[320,2,128]{2,0,1:T(8,128)} fusion(f32[320,2,128]{2,0,1:T(8,128)} %get-tuple-element.244, pred[]{:T(512)S(6)} %compare.9, bf16[5,192,2,128]{3,1,2,0:T(8,128)(2,1)} %get-tuple-element.262, s32[]{:T(128)S(6)} %copy.36, f32[2,192]{1,0:T(2,128)S(1)} %get-tuple-element.226, bf16[320,2,128]{2,0,1:T(8,128)(2,1)} %get-tuple-element.261, ...), kind=kOutput, calls=%fused_computation.10.clone.1 | convolution fusion | flops 63693504 | bytes 1080320 | tf_op jit(solution)/shard_map/while/body/eval_jaxpr/grk,rgd->kgd/dot_general | solution.py:95
  87.7 1.2 fusion.112
  88.9 1.8 %fusion.114 = bf16[5,192,2,128]{3,1,2,0:T(8,128)(2,1)} fusion(bf16[5,192,2,128]{3,1,2,0:T(8,128)(2,1)} %get-tuple-element.245, s32[]{:T(128)S(6)} %copy.36, bf16[2,192,320]{2,1,0:T(8,128)(2,1)S(1)} %fusion.111, bf16[320,2,128]{2,0,1:T(8,128)(2,1)} %get-tuple-element.261), kind=kOutput, calls=%fused_computation.20.clone.1 | convolution fusion | flops 31555584 | bytes 507908 | tf_op jit(solution)/shard_map/while/body/eval_jaxpr/grk,kgd->rgd/dot_general | solution.py:87
  90.7 1.0 bitcast_dynamic-update-slice_fusion
  94.0 1.7 %collective-permute-start = (f32[1,32,512]{2,1,0:T(8,128)S(1)}, f32[1,32,512]{2,1,0:T(8,128)S(1)}, u32[]{:S(2)}, u32[]{:S(2)}) collective-permute-start(f32[1,32,512]{2,1,0:T(8,128)S(1)} %select_bitcast_fusion), channel_id=1, source_target_pairs={{0,4},{4,0},{8,12},{12,8},{1,5},{5,1},{9,13},{13,9},{2,6},{6,2},{1... | collective-permute-start | bytes 196616 | tf_op jit(solution)/shard_map/ppermute | solution.py:11
  95.8 1.0 slice.121
  96.7 1.9 %collective-permute-done.1 = f32[2,32,512]{2,1,0:T(8,128)S(1)} collective-permute-done((f32[2,32,512]{2,1,0:T(8,128)S(1)}, f32[2,32,512]{2,1,0:T(8,128)S(1)}, u32[]{:S(2)}, u32[]{:S(2)}) %collective-permute-start.1) | collective-permute-done | bytes 131104 | tf_op jit(solution)/shard_map/ppermute | solution.py:11
  99.7 3.0 %collective-permute-done.2 = f32[1,32,512]{2,1,0:T(8,128)S(1)} collective-permute-done((f32[1,32,512]{2,1,0:T(8,128)S(1)}, f32[1,32,512]{2,1,0:T(8,128)S(1)}, u32[]{:S(2)}, u32[]{:S(2)}) %collective-permute-start.2) | collective-permute-done | bytes 65568 | tf_op jit(solution)/shard_map/ppermute | solution.py:11
  102.7 1.0 fusion.50
  104.4 2.3 %fusion.48 = bf16[192,5120]{1,0:T(8,128)(2,1)} fusion(f32[192,5120]{1,0:T(8,128)S(1)} %fusion.50, bf16[5120,256]{1,0:T(8,128)(2,1)S(1)} %copy-done.1, bf16[192,512]{1,0:T(8,128)(2,1)S(1)} %pad_maximum_fusion.1), kind=kOutput, calls=%fused_computation.41 | convolution fusion | flops 505282560 | bytes 8617984 | tf_op jit(solution)/shard_map/dot_general | solution.py:132
  106.8 1.3 copy.18
  108.1 1.0 copy.21
  109.1 32.2 %reduce-scatter.2.cloned.1.call-done = bf16[48,5120]{1,0:T(8,128)(2,1)} async-done(((bf16[192,5120]{1,0:T(8,128)(2,1)}), bf16[48,5120]{1,0:T(8,128)(2,1)}) %reduce-scatter.2.cloned.1.call-update) | async-done | bytes 491536 | tf_op jit(solution)/shard_map/reduce_scatter | solution.py:135
  (51 shorter events, 7.5 us)
Async XLA Ops:
  7.2 95.5 %copy-start = (bf16[5120,256]{1,0:T(8,128)(2,1)S(1)}, bf16[5120,256]{1,0:T(8,128)(2,1)}, u32[]{:S(2)}) copy-start(bf16[5120,256]{1,0:T(8,128)(2,1)} %param.13) | copy-start | bytes 7864324
  7.2 16.9 %copy-start.7 = (pred[192]{0:T(512)(128)(4,1)S(1)}, pred[192]{0:T(512)(128)(4,1)}, u32[]{:S(2)}) copy-start(pred[192]{0:T(512)(128)(4,1)} %constant.81.clone.1) | copy-start | bytes 580
  7.2 134.0 %reduce-scatter.2.cloned.1.call-start = ((), (), s32[]{:S(2)}) async-start(), calls=%async_computation.1 | async-start | bytes 2457600 | tf_op jit(solution)/shard_map/reduce_scatter | solution.py:135
  25.3 8.3 %copy-start.5 = (s32[320]{0:T(512)S(1)}, s32[320]{0:T(512)}, u32[]{:S(2)}) copy-start(s32[320]{0:T(512)} %constant.83.clone.1) | copy-start | bytes 3844
  25.3 8.3 %copy-start.6 = (s32[192]{0:T(256)S(1)}, s32[192]{0:T(256)}, u32[]{:S(2)}) copy-start(s32[192]{0:T(256)} %constant.84.clone.1) | copy-start | bytes 2308
  26.4 6.4 %copy-start.3 = (bf16[40,2,8,128]{3,2,1,0:T(8,128)(2,1)S(1)}, bf16[40,2,8,128]{3,2,1,0:T(8,128)(2,1)}, u32[]{:S(2)}) copy-start(bf16[40,2,8,128]{3,2,1,0:T(8,128)(2,1)} %get-tuple-element.143) | copy-start | bytes 491524
  26.4 6.4 %copy-start.4 = (bf16[40,2,8,128]{3,2,1,0:T(8,128)(2,1)S(1)}, bf16[40,2,8,128]{3,2,1,0:T(8,128)(2,1)}, u32[]{:S(2)}) copy-start(bf16[40,2,8,128]{3,2,1,0:T(8,128)(2,1)} %get-tuple-element.144) | copy-start | bytes 491524
  91.7 0.9 copy-start.2
  92.6 6.0 %collective-permute-start.1 = (f32[2,32,512]{2,1,0:T(8,128)S(1)}, f32[2,32,512]{2,1,0:T(8,128)S(1)}, u32[]{:S(2)}, u32[]{:S(2)}) collective-permute-start(f32[2,32,512]{2,1,0:T(8,128)S(1)} %bitcast.151), channel_id=1, source_target_pairs={{0,8},{4,12},{8,0},{12,4},{1,9},{5,13},{9,1},{13,5},{2,10},{6,14},... | collective-permute-start | bytes 393224 | tf_op jit(solution)/shard_map/ppermute | solution.py:11
  94.0 4.8 %collective-permute-start = (f32[1,32,512]{2,1,0:T(8,128)S(1)}, f32[1,32,512]{2,1,0:T(8,128)S(1)}, u32[]{:S(2)}, u32[]{:S(2)}) collective-permute-start(f32[1,32,512]{2,1,0:T(8,128)S(1)} %select_bitcast_fusion), channel_id=1, source_target_pairs={{0,4},{4,0},{8,12},{12,8},{1,5},{5,1},{9,13},{13,9},{2,6},{6,2},{1... | collective-permute-start | bytes 196616 | tf_op jit(solution)/shard_map/ppermute | solution.py:11
  98.7 4.0 %collective-permute-start.2 = (f32[1,32,512]{2,1,0:T(8,128)S(1)}, f32[1,32,512]{2,1,0:T(8,128)S(1)}, u32[]{:S(2)}, u32[]{:S(2)}) collective-permute-start(f32[1,32,512]{2,1,0:T(8,128)S(1)} %slice_select_fusion.2), channel_id=1, source_target_pairs={{0,4},{4,0},{8,12},{12,8},{1,5},{5,1},{9,13},{13,9},{2,6},{6,2},{1... | collective-permute-start | bytes 196616 | tf_op jit(solution)/shard_map/ppermute | solution.py:11
  102.7 1.7 %copy-start.1 = (bf16[5120,256]{1,0:T(8,128)(2,1)S(1)}, bf16[5120,256]{1,0:T(8,128)(2,1)}, u32[]{:S(2)}) copy-start(bf16[5120,256]{1,0:T(8,128)(2,1)} %param.14) | copy-start | bytes 7864324
Sparse Core Ops, SparseCore 0:
  106.9 34.2 reduce-scatter.1
where the time goes:
time: 150 us; the launch traced here: 148 us
  matrix products  59.5 us (40%)
  waiting for transfers between devices  37.1 us (25%)
  local copies, waits for them, and re-layouts  16.8 us (11%)
  between operations  14.9 us (10%)
  blocking collectives  13.3 us (9%)
  other arithmetic  3.91 us (3%)
  starting transfers between devices  2.37 us (2%)
    reduce_scatter x1, waiting for transfers between devices, local(): lax.psum_scatter((key_term + value_term).astype(jnp.bfloat16), 'head', sc...  32.2 us
    dot_general x5, matrix products, one_head(): jnp.einsum('grk,rgd->kgd', attn_bf, d_one, preferred_element_type=jnp.flo...  14.2 us
    all_gather x1, blocking collectives, local(): gathered = lax.all_gather(own_anc, 'branch', axis=0, tiled=True)  13.3 us
    unnamed x24, local copies, waits for them, and re-layouts  11.5 us
    sub x5, matrix products, one_head(): exp_scores = jnp.exp(scores - row_max)  10.7 us
    dot_general x5, matrix products, one_head(): jnp.einsum('grk,kgd->rgd', attn_bf, value_part, preferred_element_type=jn...  9.55 us
    dot_general x5, matrix products, one_head(): jnp.einsum('grk,kgd->rgd', grad_score, key_part, preferred_element_type=j...  8.94 us
    dot_general x5, matrix products, one_head(): jnp.einsum('rgd,kgd->grk', d_one, value_part, preferred_element_type=jnp....  6.86 us
  transfers between devices with their start and end apart: 4, of which 3 were waited for; matrix products, arithmetic and copies ran while one was open for 3% of the time, Pallas kernels for 0%

commit v1 on v0

v1 whole, which is shorter than its diff:
```python
import functools
import math

import jax
import jax.numpy as jnp
from jax import lax
from jax.experimental import pallas as pl
from jax.experimental.pallas import tpu as pltpu
from jax.sharding import PartitionSpec as P

HD = 128
ANC = 32
NEG = -1e30
NT = (((1,), (1,)), ((), ()))
NN = (((1,), (0,)), ((), ()))
BF = jnp.bfloat16
F32 = jnp.float32


def dot(a, b, dims):
    return lax.dot_general(a, b, dims, preferred_element_type=F32)


def flipped(value, mask):
    out = value
    for bit in range(mask.bit_length()):
        if mask >> bit & 1:
            out = out + (1 - 2 * lax.rem(lax.div(value, 1 << bit), 2)) * (1 << bit)
    return out


class Plan:
    def __init__(self, branch, head, rows, kv_cols, q_cols, width):
        self.branch, self.head, self.rows = branch, head, rows
        self.levels = branch.bit_length() - 1
        self.leaf = rows - self.levels * ANC
        self.kv_cols, self.q_cols, self.width = kv_cols, q_cols, width
        self.kv = kv_cols // HD
        self.group = q_cols // kv_cols
        self.off = {}
        at = 0
        for level in range(self.levels, 0, -1):
            self.off[level] = at
            at += 2**level * ANC
        self.anc_keys = at
        self.keys = at + self.leaf
        self.anc_rows = self.levels * ANC
        self.together = self.group if self.keys <= 512 else 1
        self.lanes = -(-self.together * self.anc_rows // 128) * 128
        self.chunk = rows // head
        self.padded = -(-self.chunk // 16) * 16
        self.half = width // 2
        self.moves = [(l, d) for l in range(self.levels, 0, -1) for d in range(1, 2**l)]
        if self.padded == self.chunk:
            bounds = [(0, self.leaf), (self.leaf, rows)]
        else:
            bounds = [(0, head * self.padded)]
        self.phases = []
        count = 0
        for low, high in bounds:
            segs = []
            for j in range(head):
                a, b = max(low, j * self.padded), min(high, (j + 1) * self.padded)
                if a < b:
                    segs.append((count, j, a - j * self.padded, b - j * self.padded, a - low))
                    count += 1
            self.phases.append((low, high, segs))
        self.seg_count = count
        self.tiles = 2
        self.tile = self.half // self.tiles


def kernel(pn, len_ref, q_hbm, k_hbm, v_hbm, c_hbm, kw_hbm, vw_hbm, dq_hbm, di_hbm,
           qv, cv, kall, vall, kwv, vwv, dsl, pbl, dsa, pba, sendg, recvg, gr, gpad,
           psend, mrecv, psum, xrecv, dqv, outv,
           in_sem, own_sem, w_sem, ks_sem, kr_sem, gs_sem, gr_sem, ms_sem, mr_sem,
           xs_sem, xr_sem, out_sem):
    b = lax.axis_index("branch")
    me = lax.axis_index("head")
    core = lax.rem(me, 2)
    chip = lax.div(me, 2)
    mate = me + 1 - 2 * core
    leaf, anc, keys, group = pn.leaf, pn.anc_keys, pn.keys, pn.group
    scale = HD ** (-0.5)

    local = [
        pltpu.make_async_copy(q_hbm, qv, in_sem.at[0]),
        pltpu.make_async_copy(c_hbm, cv, in_sem.at[1]),
        pltpu.make_async_copy(k_hbm.at[pl.ds(0, leaf)], kall.at[pl.ds(anc, leaf)], in_sem.at[2]),
        pltpu.make_async_copy(v_hbm.at[pl.ds(0, leaf)], vall.at[pl.ds(anc, leaf)], in_sem.at[3]),
    ]
    for l in range(1, pn.levels + 1):
        src = pl.ds(leaf + (l - 1) * ANC, ANC)
        dst = pl.ds(pn.off[l], ANC)
        local.append(pltpu.make_async_copy(k_hbm.at[src], kall.at[dst], own_sem.at[0, l - 1]))
        local.append(pltpu.make_async_copy(v_hbm.at[src], vall.at[dst], own_sem.at[1, l - 1]))
    for copy in local:
        copy.start()
    weights = [
        pltpu.make_async_copy(kw_hbm, kwv, w_sem.at[0]),
        pltpu.make_async_copy(vw_hbm, vwv, w_sem.at[1]),
    ]

    barrier = pltpu.get_barrier_semaphore()
    for d in range(1, pn.branch):
        pl.semaphore_signal(barrier, inc=1, device_id={"branch": flipped(b, d)},
                            device_id_type=pl.DeviceIdType.MESH)
    for e in range(1, pn.head):
        pl.semaphore_signal(barrier, inc=1, device_id={"head": lax.rem(me + e, pn.head)},
                            device_id_type=pl.DeviceIdType.MESH)
    pl.semaphore_wait(barrier, pn.branch - 1 + pn.head - 1)

    gathers = []
    for no, (l, d) in enumerate(pn.moves):
        src = pl.ds(leaf + (l - 1) * ANC, ANC)
        dst = pl.ds(pn.off[l] + d * ANC, ANC)
        for which, (hbm, ref) in enumerate(((k_hbm, kall), (v_hbm, vall))):
            copy = pltpu.make_async_remote_copy(
                src_ref=hbm.at[src], dst_ref=ref.at[dst],
                send_sem=ks_sem.at[which, no], recv_sem=kr_sem.at[which, no],
                device_id={"branch": flipped(b, d)}, device_id_type=pl.DeviceIdType.MESH)
            copy.start()
            gathers.append(copy)
    for copy in weights:
        copy.start()

    live = lax.broadcasted_iota(jnp.int32, (leaf, HD), 0) < len_ref[0]
    causal = (lax.broadcasted_iota(jnp.int32, (leaf, leaf), 0)
              <= lax.broadcasted_iota(jnp.int32, (leaf, leaf), 1))
    lane = lax.broadcasted_iota(jnp.int32, (ANC, pn.lanes), 1)
    row = lax.broadcasted_iota(jnp.int32, (ANC, pn.lanes), 0)
    block = lax.shift_right_logical(lane, 5)
    wraps = jnp.zeros_like(block)
    for m in range(1, pn.together):
        wraps = wraps + jnp.where(block >= m * pn.levels, 1, 0)
    q_level = block - pn.levels * wraps + 1
    q_place = lane - 32 * block
    bias = []
    for l in range(pn.levels, 0, -1):
        for d in range(2**l):
            if d == 0:
                ok = (q_level < l) | ((q_level == l) & (row <= q_place))
            else:
                bit = lax.rem(lax.div(b, 1 << (d.bit_length() - 1)), 2)
                ok = q_level < l + bit
            bias.append(jnp.where(ok, 0.0, NEG).astype(F32))
    bias = jnp.concatenate(bias, axis=0)

    for copy in local:
        copy.wait()
    for copy in gathers:
        copy.wait_recv()

    def soft(scores, grad_prob):
        top = jnp.max(scores, axis=0, keepdims=True)
        e = jnp.exp2((scores - top) * (scale * math.log2(math.e)))
        p = e * (1.0 / jnp.sum(e, axis=0, keepdims=True))
        pb = p.astype(BF)
        delta = jnp.sum(pb.astype(F32) * grad_prob, axis=0, keepdims=True)
        return pb, (p * (grad_prob - delta)).astype(BF)

    sends = []
    for g in range(pn.kv):
        cols = slice(g * HD, (g + 1) * HD)
        kg, vg = kall[:, cols], vall[:, cols]
        kt = kg.astype(F32).T.astype(BF)
        ql, dl, qa, da = [], [], [], []
        for h in range(group):
            hc = slice((g * group + h) * HD, (g * group + h + 1) * HD)
            q = qv[0:leaf, hc]
            d = jnp.where(live, cv[0:leaf, hc].astype(F32), 0.0).astype(BF)
            ql.append(q)
            dl.append(d)
            qa.append(qv[leaf:, hc])
            da.append(cv[leaf:, hc])
            st = dot(kg, q, NT)
            gp = dot(vg, d, NT)
            st = jnp.concatenate([st[:anc], jnp.where(causal, st[anc:], NEG)], axis=0)
            pb, ds = soft(st, gp)
            pbl[:, h * leaf:(h + 1) * leaf] = pb
            dsl[:, h * leaf:(h + 1) * leaf] = ds
        pad = pn.lanes - pn.together * pn.anc_rows
        zeros = [jnp.zeros((pad, HD), BF)] if pad else []
        qs, dd = [], []
        for start in range(0, group, pn.together):
            qx = jnp.concatenate(qa[start:start + pn.together] + zeros, axis=0)
            dx = jnp.concatenate(da[start:start + pn.together] + zeros, axis=0)
            qs.append(qx)
            dd.append(dx)
            pb, ds = soft(dot(kg[:anc], qx, NT) + bias, dot(vg[:anc], dx, NT))
            at = start // pn.together * pn.lanes
            pba[:, at:at + pn.lanes] = pb
            dsa[:, at:at + pn.lanes] = ds
        ql = jnp.concatenate(ql, axis=0)
        dl = jnp.concatenate(dl, axis=0)
        qs = jnp.concatenate(qs, axis=0)
        dd = jnp.concatenate(dd, axis=0)
        gk = (dot(dsl[:anc], ql, NN) + dot(dsa[...], qs, NN)) * scale
        gv = dot(pbl[:anc], dl, NN) + dot(pba[...], dd, NN)
        sendg[g, :, 0:HD] = gk.astype(BF)
        sendg[g, :, HD:2 * HD] = gv.astype(BF)
        for no, (l, d) in enumerate(pn.moves):
            where = pl.ds(pn.off[l] + d * ANC, ANC)
            copy = pltpu.make_async_remote_copy(
                src_ref=sendg.at[g, where], dst_ref=recvg.at[g, where],
                send_sem=gs_sem.at[g, no], recv_sem=gr_sem.at[g, no],
                device_id={"branch": flipped(b, d)}, device_id_type=pl.DeviceIdType.MESH)
            copy.start()
            sends.append(copy)
        kc = slice(g * HD, (g + 1) * HD)
        vc = slice(pn.kv_cols + g * HD, pn.kv_cols + (g + 1) * HD)
        for l in range(1, pn.levels + 1):
            rows = slice(leaf + (l - 1) * ANC, leaf + l * ANC)
            gr[rows, kc] = gk[pn.off[l]:pn.off[l] + ANC]
            gr[rows, vc] = gv[pn.off[l]:pn.off[l] + ANC]
        gr[0:leaf, kc] = dot(dsl[anc:], ql, NN) * scale
        gr[0:leaf, vc] = dot(pbl[anc:], dl, NN)
        dq = dot(kt, dsl[...], NN)
        for h in range(group):
            hc = slice((g * group + h) * HD, (g * group + h + 1) * HD)
            dqv[0:leaf, hc] = (dq[:, h * leaf:(h + 1) * leaf].T * scale).astype(BF)
        dqa = (dot(kt[:, :anc], dsa[...], NN).T * scale).astype(BF)
        for h in range(group):
            hc = slice((g * group + h) * HD, (g * group + h + 1) * HD)
            at = h // pn.together * pn.lanes + h % pn.together * pn.anc_rows
            dqv[leaf:, hc] = dqa[at:at + pn.anc_rows]

    dq_out = pltpu.make_async_copy(dqv, dq_hbm, out_sem.at[0])
    dq_out.start()
    for copy in weights:
        copy.wait()

    mine0 = core * pn.half
    other0 = (1 - core) * pn.half

    def reduce_anc():
        for copy in sends:
            copy.wait_recv()
        for g in range(pn.kv):
            for l in range(1, pn.levels + 1):
                rows = slice(leaf + (l - 1) * ANC, leaf + l * ANC)
                total = recvg[g, pn.off[l] + ANC:pn.off[l] + 2 * ANC].astype(F32)
                for d in range(2, 2**l):
                    at = pn.off[l] + d * ANC
                    total = total + recvg[g, at:at + ANC].astype(F32)
                kc = slice(g * HD, (g + 1) * HD)
                vc = slice(pn.kv_cols + g * HD, pn.kv_cols + (g + 1) * HD)
                gr[rows, kc] = gr[rows, kc] + total[:, :HD]
                gr[rows, vc] = gr[rows, vc] + total[:, HD:]

    waits = []
    exchanges = []
    for phase, (low, high, segs) in enumerate(pn.phases):
        if phase == len(pn.phases) - 1:
            reduce_anc()
        if pn.padded == pn.chunk:
            grads = gr[low:high]
        else:
            gpad[...] = jnp.zeros_like(gpad)
            for j in range(pn.head):
                gpad[j * pn.padded:j * pn.padded + pn.chunk] = gr[j * pn.chunk:(j + 1) * pn.chunk]
            grads = gpad[...]
        grads = grads.astype(BF)
        gk, gv = grads[:, :pn.kv_cols], grads[:, pn.kv_cols:]

        def part(start):
            rows = pl.ds(pl.multiple_of(start, 128), pn.tile)
            return (dot(gk, kwv[rows, :], NT) + dot(gv, vwv[rows, :], NT)).astype(BF)

        mates = []
        for t in range(pn.tiles):
            where = (pl.ds(low, high - low), pl.ds(t * pn.tile, pn.tile))
            psend[low:high, t * pn.tile:(t + 1) * pn.tile] = part(other0 + t * pn.tile)
            copy = pltpu.make_async_remote_copy(
                src_ref=psend.at[where], dst_ref=mrecv.at[where],
                send_sem=ms_sem.at[phase, t], recv_sem=mr_sem.at[phase, t],
                device_id={"head": mate}, device_id_type=pl.DeviceIdType.MESH)
            copy.start()
            mates.append(copy)
            waits.append(copy)
        for t in range(pn.tiles):
            mine = part(mine0 + t * pn.tile).astype(F32)
            mates[t].wait_recv()
            tc = slice(t * pn.tile, (t + 1) * pn.tile)
            both = (mine + mrecv[low:high, tc].astype(F32)).astype(BF)
            for no, j, r0, r1, at in segs:
                psum[j, r0:r1, tc] = both[at:at + r1 - r0]
                where = (pl.ds(r0, r1 - r0), pl.ds(t * pn.tile, pn.tile))
                copy = pltpu.make_async_remote_copy(
                    src_ref=psum.at[(j,) + where], dst_ref=xrecv.at[(me,) + where],
                    send_sem=xs_sem.at[no, t], recv_sem=xr_sem.at[me, no, t],
                    device_id={"head": j}, device_id_type=pl.DeviceIdType.MESH)
                exchanges.append((j, copy))

                @pl.when(me != j)
                def _(copy=copy):
                    copy.start()

    for phase, (low, high, segs) in enumerate(pn.phases):
        for t in range(pn.tiles):
            for no, j, r0, r1, at in segs:
                @pl.when(me == j)
                def _(no=no, j=j, r0=r0, r1=r1, t=t):
                    where = (pl.ds(r0, r1 - r0), pl.ds(t * pn.tile, pn.tile))
                    for e in range(1, pn.head):
                        peer = lax.rem(me + e, pn.head)
                        pltpu.make_async_remote_copy(
                            src_ref=psum.at[(j,) + where], dst_ref=xrecv.at[(peer,) + where],
                            send_sem=xs_sem.at[no, t], recv_sem=xr_sem.at[peer, no, t],
                            device_id={"head": peer},
                            device_id_type=pl.DeviceIdType.MESH).wait_recv()

    chips = pn.head // 2
    own = psum[me].astype(F32)
    for e in range(1, chips):
        own = own + xrecv[2 * lax.rem(chip + e, chips) + core].astype(F32)
    outv[0] = own[:pn.chunk].astype(BF)
    rest = xrecv[mate].astype(F32)
    for e in range(1, chips):
        rest = rest + xrecv[2 * lax.rem(chip + e, chips) + 1 - core].astype(F32)
    outv[1] = rest[:pn.chunk].astype(BF)
    outs = [
        pltpu.make_async_copy(
            outv.at[i], di_hbm.at[:, pl.ds(pl.multiple_of(start, 128), pn.half)], out_sem.at[1 + i])
        for i, start in enumerate((mine0, other0))
    ]
    for copy in outs:
        copy.start()
    for copy in gathers + sends + waits:
        copy.wait_send()
    for j, copy in exchanges:
        @pl.when(me != j)
        def _(copy=copy):
            copy.wait_send()
    dq_out.wait()
    for copy in outs:
        copy.wait()


def solution(mesh):
    branch, head = mesh.shape["branch"], mesh.shape["head"]

    def local(queries, key_states, value_states, cotangent, key_weight, value_weight, leaf_length):
        rows, q_cols = queries.shape
        kv_cols, width = key_states.shape[1], key_weight.shape[0]
        pn = Plan(branch, head, rows, kv_cols, q_cols, width)
        hbm = pl.BlockSpec(memory_space=pl.ANY)
        vm = pltpu.VMEM
        dma = pltpu.SemaphoreType.DMA
        total = pn.head * pn.padded
        anc_cols = pn.group // pn.together * pn.lanes
        n = len(pn.moves)
        scratch = [
            vm((rows, q_cols), BF), vm((rows, q_cols), BF),
            vm((pn.keys, kv_cols), BF), vm((pn.keys, kv_cols), BF),
            vm((width, kv_cols), BF), vm((width, kv_cols), BF),
            vm((pn.keys, pn.group * pn.leaf), BF), vm((pn.keys, pn.group * pn.leaf), BF),
            vm((pn.anc_keys, anc_cols), BF), vm((pn.anc_keys, anc_cols), BF),
            vm((pn.kv, pn.anc_keys, 2 * HD), BF), vm((pn.kv, pn.anc_keys, 2 * HD), BF),
            vm((rows, 2 * kv_cols), F32),
            vm((total, 2 * kv_cols) if pn.padded != pn.chunk else (8, 128), F32),
            vm((total, pn.half), BF), vm((total, pn.half), BF),
            vm((head, pn.padded, pn.half), BF), vm((head, pn.padded, pn.half), BF),
            vm((rows, q_cols), BF), vm((2, pn.chunk, pn.half), BF),
            dma((4,)), dma((2, pn.levels)), dma((2,)),
            dma((2, n)), dma((2, n)), dma((pn.kv, n)), dma((pn.kv, n)),
            dma((len(pn.phases), pn.tiles)), dma((len(pn.phases), pn.tiles)),
            dma((pn.seg_count, pn.tiles)), dma((head, pn.seg_count, pn.tiles)),
            dma((3,)),
        ]
        return pl.pallas_call(
            functools.partial(kernel, pn),
            out_shape=(
                jax.ShapeDtypeStruct((rows, q_cols), BF),
                jax.ShapeDtypeStruct((pn.chunk, width), BF),
            ),
            in_specs=[pl.BlockSpec(memory_space=pltpu.SMEM)] + [hbm] * 6,
            out_specs=(hbm, hbm),
            scratch_shapes=scratch,
            compiler_params=pltpu.CompilerParams(
                collective_id=0, has_side_effects=True, vmem_limit_bytes=60 * 2**20
            ),
        )(leaf_length, queries, key_states, value_states, cotangent, key_weight, value_weight)

    placed = (
        P(("groups", "branch"), "head"),
        P(("groups", "branch"), "head"),
        P(("groups", "branch"), "head"),
        P(("groups", "branch"), "head"),
        P(None, "head"),
        P(None, "head"),
        P(("groups", "branch")),
    )
    return jax.shard_map(
        local,
        mesh=mesh,
        in_specs=placed,
        out_specs=(P(("groups", "branch"), "head"), P(("groups", "branch", "head"), None)),
        check_vma=False,
    )
```

time: 150 us -> 34 us (0.23); the launches traced: 148 us -> 33.8 us
  matrix products: 59.5 us -> 0 us
  waiting for transfers between devices: 37.1 us -> 0 us
  Pallas kernels: 0 us -> 28.9 us
  between operations: 14.9 us -> 1.29 us
  blocking collectives: 13.3 us -> 0 us
  local copies, waits for them, and re-layouts: 16.8 us -> 3.68 us
  other arithmetic: 3.91 us -> 0 us
  starting transfers between devices: 2.37 us -> 0 us
    dot_general x27 -> x0, matrix products: 48.8 us -> none  [the longest x5 14.2 us: one_head(): jnp.einsum('grk,rgd->kgd', attn_bf, d_one, preferred_element_type=jnp.flo...]
    reduce_scatter x1 -> x0, waiting for transfers between devices: 32.2 us -> none  [local(): lax.psum_scatter((key_term + value_term).astype(jnp.bfloat16), 'head', sc...]
    pallas_call x0 -> x1, Pallas kernels: none -> 28.9 us  [local(): pl.pallas_call(functools.partial(kernel, pn), out_shape=(jax.ShapeDtypeSt...]
    all_gather x1 -> x0, blocking collectives: 13.3 us -> none  [local(): gathered = lax.all_gather(own_anc, 'branch', axis=0, tiled=True)]
    sub x5 -> x0, matrix products: 10.7 us -> none  [one_head(): exp_scores = jnp.exp(scores - row_max)]
    unnamed x24 -> x2, local copies, waits for them, and re-layouts: 11.5 us -> 3.68 us
    ppermute x3 -> x0, waiting for transfers between devices: 4.9 us -> none  [swapped(): lax.ppermute(value, axis, [(i, i ^ 1 << apart) for i in range(lax.axis_si...]
    ppermute x3 -> x0, starting transfers between devices: 2.34 us -> none  [swapped(): lax.ppermute(value, axis, [(i, i ^ 1 << apart) for i in range(lax.axis_si...]
  transfers between devices with their start and end apart: 4 -> 0, of which waited for: 3 -> 0; matrix products, arithmetic and copies ran while one was open for 3% -> 0% of each run, Pallas kernels for 0% -> 0%
where the time goes in v1:
time: 34 us; the launch traced here: 33.8 us
  Pallas kernels  28.9 us (85%)
  local copies, waits for them, and re-layouts  3.68 us (11%)
  between operations  1.29 us (4%)
    pallas_call x1, Pallas kernels, local(): pl.pallas_call(functools.partial(kernel, pn), out_shape=(jax.ShapeDtypeSt...  28.9 us
    unnamed x2, local copies, waits for them, and re-layouts  3.68 us

profile of v1, /device:TPU:1, one launch (start us, length us, event | category | flops | bytes accessed | tf_op | source)
XLA Modules:
  0.0 33.8 jit_solution(18023382502025425799)
XLA Ops:
  1.3 28.9 %shard_map.86 = (bf16[192,1280]{1,0:T(8,128)(2,1)}, bf16[48,5120]{1,0:T(8,128)(2,1)}) custom-call(s32[1]{0:T(128)S(6)} %copy.11.len_ref, bf16[192,1280]{1,0:T(8,128)(2,1)} %q_hbm.1, bf16[192,256]{1,0:T(8,128)(2,1)} %k_hbm.1, bf16[192,256]{1,0:T(8,128)(2,1)} %v_hbm.1, bf16[192,1280]{1,0:T(8,128)(2,1)} %c_hbm.1, bf16[5120,256]{1,0:T(8,128)(2,1)} %kw_hbm.1, ...), custom_call_target="tpu_custom_call" | custom-call | tf_op jit(solution)/shard_map/pallas_call | solution.py:371
  30.1 1.8 %copy.12 = bf16[192,1280]{1,0:T(8,128)(2,1)} copy(bf16[192,1280]{1,0:T(8,128)(2,1)} %get-tuple-element.4) | data formatting | bytes 983040
  32.0 1.8 %copy.13 = bf16[48,5120]{1,0:T(8,128)(2,1)} copy(bf16[48,5120]{1,0:T(8,128)(2,1)} %get-tuple-element.5) | data formatting | bytes 983040
